TPU v7x, 256 devices: a whole 4x4x8 slice. The times are simulated.
256 devices in a mesh: prompt: 8 (over x, y_lo), tensor: 32 (over z, y_hi, core).
Axes of the slice: x: 4, y: 4 (y_hi: 2, y_lo: 2; y = y_hi * 2 + y_lo), z: 8, core: 2. Of those that a mesh axis runs over, the one named last changes fastest.
Arguments:
- tokens: bfloat16 [8, 128, 8192], P('prompt')
- gate_weight: bfloat16 [8192, 28672], P('prompt', 'tensor'), may hold values from -0.0625 to 0.0625
- up_weight: bfloat16 [8192, 28672], P('prompt', 'tensor'), may hold values from -0.0625 to 0.0625
- down_weight: bfloat16 [28672, 8192], P('tensor', 'prompt')
- norm_gain: float32 [8192], P('prompt'), may hold values from 0.1 to 1.9
- unembed: bfloat16 [8192, 86016], P('prompt', 'tensor'), may hold values from -0.5 to 0.5
- guidance: float32 [8], replicated, may hold values from -1.5 to 2.5
- logit_bias: float32 [128, 86016], P('prompt', 'tensor'), may hold values from -2 to 322
Outputs:
- log_probs: float32 [128, 86016], P('prompt', 'tensor')
All inputs are finite; a program needn't handle non-finite values.
Results may differ from a plain program's by a relative error of at most 0.0025.
Values may be sent and summed in bfloat16 or wider, within the bound.
No kernel may reach another device: no remote copies, remote signals or barrier semaphores. Data moves between devices by JAX's collectives and lax.ppermute only.
A program may use at most 64 MiB of HBM per device.

v0:
```python
import jax
import jax.numpy as jnp
from jax import lax
from jax.sharding import Mesh
from jax.sharding import PartitionSpec as P

D = 8192
PROMPT = ("prompt_0", "prompt_1")


def own_rows(so_far, axes):
    for axis in axes:
        so_far = lax.psum_scatter(so_far, axis, scatter_dimension=0, tiled=True)
    return so_far


def copy_for_each(array, axis):
    peers = lax.axis_size(axis)
    return lax.all_to_all(
        jnp.broadcast_to(array[None], (peers, *array.shape)), axis, 0, 0, tiled=True
    )


def joined_along(tiles, dim):
    tiles = jnp.moveaxis(tiles, 0, dim)
    shape = tiles.shape
    return tiles.reshape(*shape[:dim], shape[dim] * shape[dim + 1], *shape[dim + 2 :])


def collect(array, axis, dim):
    tiles = copy_for_each(array, axis)
    return joined_along(tiles, dim)


def of_everyone(array, axis):
    return copy_for_each(array, axis).sum(axis=0)


def cut_along(array, dim, peers):
    shape = array.shape
    tiles = array.reshape(*shape[:dim], peers, shape[dim] // peers, *shape[dim + 1 :])
    return jnp.moveaxis(tiles, dim, 0)


def sent_and_summed(array, axis, dim):
    tiles = cut_along(array, dim, lax.axis_size(axis))
    arrived = lax.all_to_all(tiles, axis, split_axis=0, concat_axis=0, tiled=True)
    return arrived.sum(axis=0)


def gathered_once(array, axis):
    leaves = jax.tree.leaves(array)
    turns = sorted(range(len(leaves)), key=lambda k: -leaves[k].size)
    width = (1, *leaves[turns[0]].shape)[-1]
    lines = [
        jnp.pad(leaves[k].reshape(-1), (0, -leaves[k].size % width)).reshape(-1, width)
        for k in turns
    ]
    both, at, found = (copy_for_each(jnp.concatenate(lines), axis), 0, {})
    for k, line in zip(turns, lines):
        slab = both[:, at : at + len(line)].reshape(len(both), -1)
        found[k] = slab[:, : leaves[k].size].reshape(-1, *leaves[k].shape)
        at += len(line)
    numbers = iter(range(len(leaves)))
    return jax.tree.map(lambda _: found[next(numbers)], array)


def combined_pairwise(pieces, combine):
    while len(jax.tree.leaves(pieces)[0]) > 1:
        pieces = jax.vmap(combine)(
            *(jax.tree.map(lambda part: part[side::2], pieces) for side in (0, 1))
        )
    return jax.tree.map(lambda part: part[0], pieces)


def merged(array, axis, combine):
    pieces = gathered_once(array, axis)
    return combined_pairwise(pieces, combine)


def combine_lse(first, second):
    top = jnp.maximum(first[0], second[0])
    total = first[1] * jnp.exp(first[0] - top) + second[1] * jnp.exp(second[0] - top)
    return (top, total)


def local(tokens, gate_weight, up_weight, down_weight, norm_gain, unembed, guidance, logit_bias):
    variants = lax.axis_size(PROMPT)
    rows = tokens.shape[1]
    share = gate_weight.shape[0]
    spread = lax.all_to_all(tokens, PROMPT, split_axis=2, concat_axis=0, tiled=True)
    flat = spread.reshape(variants * rows, share)
    gate_part = jnp.dot(flat, gate_weight, preferred_element_type=jnp.float32)
    up_part = jnp.dot(flat, up_weight, preferred_element_type=jnp.float32)
    gate_up = own_rows(jnp.concatenate([gate_part, up_part], axis=1), PROMPT)
    width = gate_weight.shape[1]
    hidden = (jax.nn.silu(gate_up[:, :width]) * gate_up[:, width:]).astype(jnp.bfloat16)
    partial_branch = jnp.dot(
        collect(hidden, PROMPT, 0), down_weight, preferred_element_type=jnp.float32
    )
    mine = lax.psum_scatter(partial_branch, "tensor", scatter_dimension=0, tiled=True)
    count = mine.shape[0]
    start = lax.axis_index("tensor") * count
    state = lax.dynamic_slice_in_dim(flat, start, count, 0).astype(jnp.float32) + mine
    square = of_everyone(jnp.sum(state * state, axis=1), PROMPT)
    owned = (state * lax.rsqrt(square / D + 1e-05)[:, None] * norm_gain).astype(jnp.bfloat16)
    normed = lax.all_gather(owned, "tensor", axis=0, tiled=True)
    blocks = normed.reshape(variants, rows, share)
    mixed = jnp.tensordot(guidance, blocks.astype(jnp.float32), axes=1)
    high = mixed.astype(jnp.bfloat16)
    low = (mixed - high.astype(jnp.float32)).astype(jnp.bfloat16)
    stacked = jnp.concatenate([high, low], axis=0)
    product = jnp.dot(stacked, unembed, preferred_element_type=jnp.float32)
    scores = (
        sent_and_summed(
            product[: rows // variants * lax.axis_size(PROMPT)]
            + product[rows // variants * lax.axis_size(PROMPT) :],
            PROMPT,
            0,
        )
        + logit_bias
    )
    local_top = jnp.max(scores, axis=1)
    local_total = jnp.sum(jnp.exp(scores - local_top[:, None]), axis=1)
    top, total_exp = merged((local_top, local_total), "tensor", combine_lse)
    return scores - top[:, None] - jnp.log(total_exp)[:, None]


def solution(mesh):
    finer = Mesh(
        mesh.devices.reshape(4, 2, mesh.shape["tensor"]), ("prompt_0", "prompt_1", "tensor")
    )
    placed = (
        P(PROMPT, None, None),
        P(PROMPT, "tensor"),
        P(PROMPT, "tensor"),
        P("tensor", PROMPT),
        P(PROMPT),
        P(PROMPT, "tensor"),
        P(),
        P(PROMPT, "tensor"),
    )
    return jax.shard_map(
        local, mesh=finer, in_specs=placed, out_specs=P(PROMPT, "tensor"), check_vma=False
    )
```

profile of v0, /device:TPU:1, one launch (start us, length us, event | category | flops | bytes accessed | tf_op | source)
XLA Modules:
  0.0 547.3 jit_solution(13178497889290529071)
XLA Ops:
  6.5 0.0 copy-start
  6.5 0.0 reduce-scatter.4.cloned.1.call-start
  6.5 9.6 %copy.23 = bf16[1,128,8192]{1,0,2:T(2,128)(2,1)} copy(bf16[1,128,8192]{2,1,0:T(8,128)(2,1)} %param.8) | data formatting | bytes 4194304 | tf_op args[0]
  16.2 0.5 broadcast.18
  16.7 46.5 %reduce.1 = bf16[8192,128]{1,0:T(8,128)(2,1)} reduce(bf16[8192,1,128]{2,1,0:T(2,128)(2,1)} %bitcast.47, bf16[]{:T(256)} %broadcast.18), dimensions={1}, to_apply=%bitcast.29.reduce_sub_computation | reduce | bytes 4194306
  63.2 5.8 %reshape.57 = bf16[8,2,65536]{2,1,0:T(2,128)(2,1)} reshape(bf16[8192,128]{1,0:T(8,128)(2,1)} %reduce.1) | data formatting | bytes 4194304
  69.0 31.1 %all_to_all.36 = bf16[8,2,65536]{2,1,0:T(2,128)(2,1)} all-to-all(bf16[8,2,65536]{2,1,0:T(2,128)(2,1)} %reshape.57), channel_id=1, replica_groups=mesh['prompt_0'=4,'prompt_1'=2,'tensor'=32] {'prompt_0','prompt_1'}, dimensions={0} | all-to-all | bytes 4194304 | tf_op jit(solution)/shard_map/all_to_all | solution.py:91
  100.1 6.8 %reshape.58 = bf16[8192,1,128]{2,1,0:T(2,128)(2,1)} reshape(bf16[8,2,65536]{2,1,0:T(2,128)(2,1)} %all_to_all.36) | data formatting | bytes 4194304
  106.8 3.8 copy.30
  110.6 4.0 copy.24
  114.6 4.5 fusion.15
  119.1 0.0 copy-done.1
  119.1 0.0 copy-done.5
  119.1 2.2 fusion.16
  121.3 3.7 pad_maximum_fusion
  125.0 0.0 reduce-scatter.4.cloned.1.call-update
  125.0 0.0 reduce-scatter.6.cloned.1.call-start
  125.0 78.3 %reduce-scatter.4.cloned.1.call-done = f32[256,1792]{0,1:T(8,128)} async-done(((f32[1024,1792]{0,1:T(8,128)}), f32[256,1792]{0,1:T(8,128)}) %reduce-scatter.4.cloned.1.call-update) | async-done | bytes 1835024 | tf_op jit(solution)/shard_map/reduce_scatter | solution.py:13
  203.3 0.0 reduce-scatter.6.cloned.1.call-update
  203.4 0.2 reduce-scatter.8.cloned.1.call-start
  203.6 36.1 %reduce-scatter.6.cloned.1.call-done = f32[128,1792]{0,1:T(8,128)} async-done(((f32[256,1792]{0,1:T(8,128)}), f32[128,1792]{0,1:T(8,128)}) %reduce-scatter.6.cloned.1.call-update) | async-done | bytes 917520 | tf_op jit(solution)/shard_map/reduce_scatter | solution.py:13
  239.7 1.3 fusion.7
  240.9 0.2 copy.25
  241.1 0.2 broadcast_in_dim.6
  241.4 26.5 %all_to_all.37 = bf16[8,128,896]{2,1,0:T(8,128)(2,1)S(1)} all-to-all(bf16[8,128,896]{2,1,0:T(8,128)(2,1)S(1)} %broadcast_in_dim.6), channel_id=1, replica_groups=mesh['prompt_0'=4,'prompt_1'=2,'tensor'=32] {'prompt_0','prompt_1'}, dimensions={0} | all-to-all | bytes 3670016 | tf_op jit(solution)/shard_map/all_to_all | solution.py:19
  267.9 0.0 copy-done
  267.9 4.3 fusion.17
  272.2 0.0 reduce-scatter.8.cloned.1.call-update
  272.2 0.0 all-gather.2.cloned.1.call-start
  272.3 124.4 %reduce-scatter.8.cloned.1.call-done = f32[32,1024]{1,0:T(8,128)} async-done(((f32[1024,1024]{1,0:T(8,128)}), f32[32,1024]{1,0:T(8,128)}) %reduce-scatter.8.cloned.1.call-update) | async-done | bytes 131088 | tf_op jit(solution)/shard_map/reduce_scatter | solution.py:101
  396.6 1.0 multiply_reduce_fusion
  397.7 9.7 %all_to_all.38 = f32[8,1,32]{2,1,0:T(1,128)S(1)} all-to-all(f32[8,1,32]{2,1,0:T(1,128)S(1)} %broadcast_in_dim.7), channel_id=1, replica_groups=mesh['prompt_0'=4,'prompt_1'=2,'tensor'=32] {'prompt_0','prompt_1'}, dimensions={0} | all-to-all | bytes 2048 | tf_op jit(solution)/shard_map/all_to_all | solution.py:19
  407.4 0.0 copy-done.3
  407.4 1.6 multiply_convert_fusion
  409.0 0.0 all-gather.2.cloned.1.call-update
  409.0 83.2 %all-gather.2.cloned.1.call-done = bf16[1024,1024]{1,0:T(8,128)(2,1)} async-done(((bf16[32,1024]{1,0:T(8,128)(2,1)}), bf16[1024,1024]{1,0:T(8,128)(2,1)}) %all-gather.2.cloned.1.call-update) | async-done | bytes 2097168 | tf_op jit(solution)/shard_map/all_gather | solution.py:107
  492.3 3.0 fusion
  495.3 0.1 copy.38
  495.4 0.1 fusion.6
  495.5 4.2 fusion.2
  499.7 0.1 slice_add_fusion
  499.8 0.0 copy-start.2
  499.9 22.2 %all_to_all.39 = f32[8,16,2688]{2,1,0:T(8,128)S(1)} all-to-all(f32[8,16,2688]{2,1,0:T(8,128)S(1)} %bitcast.50), channel_id=1, replica_groups=mesh['prompt_0'=4,'prompt_1'=2,'tensor'=32] {'prompt_0','prompt_1'}, dimensions={0} | all-to-all | bytes 2752512 | tf_op jit(solution)/shard_map/all_to_all | solution.py:47
  522.0 0.1 reduce_sum.38
  522.1 0.1 fusion.11
  522.3 0.2 exponential_reduce_fusion
  522.5 17.0 %all_to_all.40 = f32[32,2,16]{2,1,0:T(2,128)S(1)} all-to-all(f32[32,2,16]{2,1,0:T(2,128)S(1)} %broadcast_in_dim.8), channel_id=1, replica_groups=mesh['prompt_0'=4,'prompt_1'=2,'tensor'=32] {'tensor'}, dimensions={0} | all-to-all | bytes 8192 | tf_op jit(solution)/shard_map/all_to_all | solution.py:19
  540.0 0.8 subtract_subtract_fusion
  (33 shorter events, 0.5 us)
Async XLA Ops:
  6.5 261.4 %copy-start = (bf16[896,1024]{1,0:T(8,128)(2,1)S(1)}, bf16[896,1024]{1,0:T(8,128)(2,1)}, u32[]{:S(2)}) copy-start(bf16[896,1024]{1,0:T(8,128)(2,1)} %param.11) | copy-start | bytes 5505028
  6.5 196.8 %reduce-scatter.4.cloned.1.call-start = ((), (), s32[]{:S(2)}) async-start(), calls=%async_computation.8 | async-start | bytes 9175040 | tf_op jit(solution)/shard_map/reduce_scatter | solution.py:13
  114.6 4.5 copy-start.1
  114.6 4.5 copy-start.5
  125.0 114.7 %reduce-scatter.6.cloned.1.call-start = ((), (), s32[]{:S(2)}) async-start(), calls=%async_computation.9 | async-start | bytes 2752512 | tf_op jit(solution)/shard_map/reduce_scatter | solution.py:13
  203.4 193.3 %reduce-scatter.8.cloned.1.call-start = ((), (), s32[]{:S(2)}) async-start(), calls=%async_computation.10 | async-start | bytes 4325376 | tf_op jit(solution)/shard_map/reduce_scatter | solution.py:101
  272.2 135.2 %copy-start.3 = (f32[1024]{0:T(1024)S(1)}, f32[1024]{0:T(1024)}, u32[]{:S(2)}) copy-start(f32[1024]{0:T(1024)} %param.12) | copy-start | bytes 12292
  272.2 220.1 %copy-start.4 = (f32[8]{0:T(128)S(1)}, f32[8]{0:T(128)}, u32[]{:S(2)}) copy-start(f32[8]{0:T(128)} %param.14) | copy-start | bytes 100
  272.2 220.1 %all-gather.2.cloned.1.call-start = ((), (), s32[]{:S(2)}) async-start(), calls=%async_computation.11 | async-start | bytes 2162688 | tf_op jit(solution)/shard_map/all_gather | solution.py:107
  499.8 22.3 %copy-start.2 = (f32[16,2688]{1,0:T(8,128)S(1)}, f32[16,2688]{1,0:T(8,128)}, u32[]{:S(2)}) copy-start(f32[16,2688]{1,0:T(8,128)} %param.15) | copy-start | bytes 516100
Sparse Core Ops, SparseCore 0:
  125.1 78.1 reduce-scatter.3
  205.8 33.7 reduce-scatter.5
  272.3 124.2 reduce-scatter.7
  409.1 83.0 all-gather.1
where the time goes:
time: 548 us; the launch traced here: 547 us
  waiting for transfers between devices  322 us (59%)
  blocking collectives  106 us (19%)
  other arithmetic  55.7 us (10%)
  local copies, waits for them, and re-layouts  31.3 us (6%)
  matrix products  18.1 us (3%)
  between operations  13.3 us (2%)
    reduce_scatter x1, waiting for transfers between devices, local(): lax.psum_scatter(partial_branch, 'tensor', scatter_dimension=0, tiled=True)  124 us
    reduce_scatter x2, waiting for transfers between devices, own_rows(): so_far = lax.psum_scatter(so_far, axis, scatter_dimension=0, tiled=True)  114 us
    all_gather x1, waiting for transfers between devices, local(): normed = lax.all_gather(owned, 'tensor', axis=0, tiled=True)  83.2 us
    all_to_all x3, blocking collectives, copy_for_each(): lax.all_to_all(jnp.broadcast_to(array[None], (peers, *array.shape)), axis...  53.2 us
    unnamed x1, other arithmetic  46.5 us
    all_to_all x1, blocking collectives, local(): lax.all_to_all(tokens, PROMPT, split_axis=2, concat_axis=0, tiled=True)  31.1 us
    unnamed x17, local copies, waits for them, and re-layouts  26.5 us
    all_to_all x1, blocking collectives, sent_and_summed(): lax.all_to_all(tiles, axis, split_axis=0, concat_axis=0, tiled=True)  22.2 us
  transfers between devices with their start and end apart: 4, of which 4 were waited for; matrix products, arithmetic and copies ran while one was open for 0% of the time, Pallas kernels for 0%

commit v1 on v0

--- a/solution.py
+++ b/solution.py
@@ -104,7 +104,9 @@
     state = lax.dynamic_slice_in_dim(flat, start, count, 0).astype(jnp.float32) + mine
     square = of_everyone(jnp.sum(state * state, axis=1), PROMPT)
     owned = (state * lax.rsqrt(square / D + 1e-05)[:, None] * norm_gain).astype(jnp.bfloat16)
-    normed = lax.all_gather(owned, "tensor", axis=0, tiled=True)
+    normed = jnp.concatenate(
+        lax.all_to_all(jnp.stack([owned] * lax.axis_size("tensor")), "tensor", 0, 0), axis=0
+    )
     blocks = normed.reshape(variants, rows, share)
     mixed = jnp.tensordot(guidance, blocks.astype(jnp.float32), axes=1)
     high = mixed.astype(jnp.bfloat16)

time: 548 us -> 523 us (0.954)
  waiting for transfers between devices: 322 us -> 239 us
  blocking collectives: 106 us -> 169 us
    all_gather x1 -> x0, waiting for transfers between devices: 83.2 us -> none  [local(): normed = lax.all_gather(owned, 'tensor', axis=0, tiled=True)]
    all_to_all x0 -> x1, blocking collectives: none -> 64.3 us  [local(): lax.all_to_all(jnp.stack([owned] * lax.axis_size('tensor')), 'tensor', 0, 0)]
    unnamed x17 -> x21, local copies, waits for them, and re-layouts: 26.5 us -> 26.5 us
    unnamed x1 -> x2, other arithmetic: 46.5 us -> 46.5 us
  transfers between devices with their start and end apart: 4 -> 3, of which waited for: 4 -> 3; matrix products, arithmetic and copies ran while one was open for 0% -> 0% of each run, Pallas kernels for 0% -> 0%
where the time goes in v1:
time: 523 us; the launch traced here: 522 us
  waiting for transfers between devices  239 us (46%)
  blocking collectives  169 us (32%)
  other arithmetic  55 us (11%)
  local copies, waits for them, and re-layouts  31.6 us (6%)
  matrix products  14 us (3%)
  between operations  13.3 us (3%)
    reduce_scatter x1, waiting for transfers between devices, local(): lax.psum_scatter(partial_branch, 'tensor', scatter_dimension=0, tiled=True)  124 us
    reduce_scatter x2, waiting for transfers between devices, own_rows(): so_far = lax.psum_scatter(so_far, axis, scatter_dimension=0, tiled=True)  114 us
    all_to_all x1, blocking collectives, local(): lax.all_to_all(jnp.stack([owned] * lax.axis_size('tensor')), 'tensor', 0, 0)  64.3 us
    all_to_all x3, blocking collectives, copy_for_each(): lax.all_to_all(jnp.broadcast_to(array[None], (peers, *array.shape)), axis...  52.8 us
    unnamed x2, other arithmetic  46.5 us
    all_to_all x1, blocking collectives, local(): lax.all_to_all(tokens, PROMPT, split_axis=2, concat_axis=0, tiled=True)  31.1 us
    unnamed x21, local copies, waits for them, and re-layouts  26.5 us
    all_to_all x1, blocking collectives, sent_and_summed(): lax.all_to_all(tiles, axis, split_axis=0, concat_axis=0, tiled=True)  20.8 us
  transfers between devices with their start and end apart: 3, of which 3 were waited for; matrix products, arithmetic and copies ran while one was open for 0% of the time, Pallas kernels for 0%

profile of v1, /device:TPU:1, one launch (start us, length us, event | category | flops | bytes accessed | tf_op | source)
XLA Modules:
  0.0 522.0 jit_solution(16478993088200832191)
XLA Ops:
  6.5 0.0 copy-start
  6.5 0.0 reduce-scatter.4.cloned.1.call-start
  6.5 9.6 %copy.23 = bf16[1,128,8192]{1,0,2:T(2,128)(2,1)} copy(bf16[1,128,8192]{2,1,0:T(8,128)(2,1)} %param.8) | data formatting | bytes 4194304 | tf_op args[0]
  16.2 0.5 broadcast.20
  16.7 46.5 %reduce.1 = bf16[8192,128]{1,0:T(8,128)(2,1)} reduce(bf16[8192,1,128]{2,1,0:T(2,128)(2,1)} %bitcast.47, bf16[]{:T(256)} %broadcast.20), dimensions={1}, to_apply=%bitcast.29.reduce_sub_computation | reduce | bytes 4194306
  63.2 5.8 %reshape.55 = bf16[8,2,65536]{2,1,0:T(2,128)(2,1)} reshape(bf16[8192,128]{1,0:T(8,128)(2,1)} %reduce.1) | data formatting | bytes 4194304
  69.0 31.1 %all_to_all.41 = bf16[8,2,65536]{2,1,0:T(2,128)(2,1)} all-to-all(bf16[8,2,65536]{2,1,0:T(2,128)(2,1)} %reshape.55), channel_id=1, replica_groups=mesh['prompt_0'=4,'prompt_1'=2,'tensor'=32] {'prompt_0','prompt_1'}, dimensions={0} | all-to-all | bytes 4194304 | tf_op jit(solution)/shard_map/all_to_all | solution.py:91
  100.1 6.8 %reshape.56 = bf16[8192,1,128]{2,1,0:T(2,128)(2,1)} reshape(bf16[8,2,65536]{2,1,0:T(2,128)(2,1)} %all_to_all.41) | data formatting | bytes 4194304
  106.8 3.8 copy.30
  110.6 4.0 copy.24
  114.6 4.5 fusion.15
  119.1 0.0 copy-done.1
  119.1 0.0 copy-done.5
  119.1 2.2 fusion.16
  121.3 3.7 pad_maximum_fusion
  125.0 0.0 reduce-scatter.4.cloned.1.call-update
  125.0 0.0 reduce-scatter.6.cloned.1.call-start
  125.0 78.3 %reduce-scatter.4.cloned.1.call-done = f32[256,1792]{0,1:T(8,128)} async-done(((f32[1024,1792]{0,1:T(8,128)}), f32[256,1792]{0,1:T(8,128)}) %reduce-scatter.4.cloned.1.call-update) | async-done | bytes 1835024 | tf_op jit(solution)/shard_map/reduce_scatter | solution.py:13
  203.3 0.0 reduce-scatter.6.cloned.1.call-update
  203.4 0.2 reduce-scatter.8.cloned.1.call-start
  203.6 36.1 %reduce-scatter.6.cloned.1.call-done = f32[128,1792]{0,1:T(8,128)} async-done(((f32[256,1792]{0,1:T(8,128)}), f32[128,1792]{0,1:T(8,128)}) %reduce-scatter.6.cloned.1.call-update) | async-done | bytes 917520 | tf_op jit(solution)/shard_map/reduce_scatter | solution.py:13
  239.7 1.3 fusion.7
  240.9 0.2 copy.25
  241.1 0.2 broadcast_in_dim.6
  241.4 26.5 %all_to_all.42 = bf16[8,128,896]{2,1,0:T(8,128)(2,1)S(1)} all-to-all(bf16[8,128,896]{2,1,0:T(8,128)(2,1)S(1)} %broadcast_in_dim.6), channel_id=1, replica_groups=mesh['prompt_0'=4,'prompt_1'=2,'tensor'=32] {'prompt_0','prompt_1'}, dimensions={0} | all-to-all | bytes 3670016 | tf_op jit(solution)/shard_map/all_to_all | solution.py:19
  267.9 0.0 copy-done
  267.9 4.3 fusion.17
  272.2 0.0 reduce-scatter.8.cloned.1.call-update
  272.2 124.4 %reduce-scatter.8.cloned.1.call-done = f32[32,1024]{1,0:T(8,128)} async-done(((f32[1024,1024]{1,0:T(8,128)}), f32[32,1024]{1,0:T(8,128)}) %reduce-scatter.8.cloned.1.call-update) | async-done | bytes 131088 | tf_op jit(solution)/shard_map/reduce_scatter | solution.py:101
  396.6 1.0 multiply_reduce_fusion
  397.7 9.7 %all_to_all.43 = f32[8,1,32]{2,1,0:T(1,128)S(1)} all-to-all(f32[8,1,32]{2,1,0:T(1,128)S(1)} %broadcast_in_dim.7), channel_id=1, replica_groups=mesh['prompt_0'=4,'prompt_1'=2,'tensor'=32] {'prompt_0','prompt_1'}, dimensions={0} | all-to-all | bytes 2048 | tf_op jit(solution)/shard_map/all_to_all | solution.py:19
  407.4 1.0 multiply_convert_fusion
  408.4 0.2 stack.2
  408.6 0.0 copy-start.4
  408.6 0.0 slice-start.1
  408.7 64.3 %all_to_all.44 = bf16[32,32,1024]{2,1,0:T(8,128)(2,1)S(1)} all-to-all(bf16[32,32,1024]{2,1,0:T(8,128)(2,1)S(1)} %stack.2), channel_id=1, replica_groups=mesh['prompt_0'=4,'prompt_1'=2,'tensor'=32] {'tensor'}, dimensions={0} | all-to-all | bytes 4194304 | tf_op jit(solution)/shard_map/all_to_all | solution.py:108
  472.9 1.4 fusion
  474.3 0.1 copy.38
  474.4 0.1 fusion.6
  474.5 1.7 fusion.2
  476.2 0.1 slice_add_fusion
  476.4 0.0 copy-start.2
  476.4 20.8 %all_to_all.45 = f32[8,16,2688]{2,1,0:T(8,128)S(1)} all-to-all(f32[8,16,2688]{2,1,0:T(8,128)S(1)} %bitcast.51), channel_id=1, replica_groups=mesh['prompt_0'=4,'prompt_1'=2,'tensor'=32] {'prompt_0','prompt_1'}, dimensions={0} | all-to-all | bytes 2752512 | tf_op jit(solution)/shard_map/all_to_all | solution.py:47
  497.2 0.1 reduce_sum.38
  497.3 0.1 fusion.11
  497.5 0.2 exponential_reduce_fusion
  497.7 16.6 %all_to_all.46 = f32[32,2,16]{2,1,0:T(2,128)S(1)} all-to-all(f32[32,2,16]{2,1,0:T(2,128)S(1)} %broadcast_in_dim.8), channel_id=1, replica_groups=mesh['prompt_0'=4,'prompt_1'=2,'tensor'=32] {'tensor'}, dimensions={0} | all-to-all | bytes 8192 | tf_op jit(solution)/shard_map/all_to_all | solution.py:19
  514.7 0.8 subtract_subtract_fusion
  (37 shorter events, 0.5 us)
Async XLA Ops:
  6.5 261.4 %copy-start = (bf16[896,1024]{1,0:T(8,128)(2,1)S(1)}, bf16[896,1024]{1,0:T(8,128)(2,1)}, u32[]{:S(2)}) copy-start(bf16[896,1024]{1,0:T(8,128)(2,1)} %param.11) | copy-start | bytes 5505028
  6.5 196.8 %reduce-scatter.4.cloned.1.call-start = ((), (), s32[]{:S(2)}) async-start(), calls=%async_computation.9 | async-start | bytes 9175040 | tf_op jit(solution)/shard_map/reduce_scatter | solution.py:13
  114.6 4.5 copy-start.1
  114.6 4.5 copy-start.5
  125.0 114.7 %reduce-scatter.6.cloned.1.call-start = ((), (), s32[]{:S(2)}) async-start(), calls=%async_computation.10 | async-start | bytes 2752512 | tf_op jit(solution)/shard_map/reduce_scatter | solution.py:13
  203.4 193.3 %reduce-scatter.8.cloned.1.call-start = ((), (), s32[]{:S(2)}) async-start(), calls=%async_computation.11 | async-start | bytes 4325376 | tf_op jit(solution)/shard_map/reduce_scatter | solution.py:101
  272.2 135.2 %copy-start.3 = (f32[1024]{0:T(1024)S(1)}, f32[1024]{0:T(1024)}, u32[]{:S(2)}) copy-start(f32[1024]{0:T(1024)} %param.12) | copy-start | bytes 12292
  272.2 202.3 %slice-start = ((s8[5505024]{0:T(1024)(128)(4,1)}), s8[1310720]{0:T(1024)(128)(4,1)S(1)}, s32[]{:S(2)}) async-start(s8[5505024]{0:T(1024)(128)(4,1)} %bitcast.65), calls=%async_computation.12 | async-start | bytes 2621440
  408.6 64.3 %copy-start.4 = (f32[8]{0:T(128)S(1)}, f32[8]{0:T(128)}, u32[]{:S(2)}) copy-start(f32[8]{0:T(128)} %param.14) | copy-start | bytes 100
  408.6 65.9 %slice-start.1 = ((s8[5505024]{0:T(1024)(128)(4,1)}), s8[4194304]{0:T(1024)(128)(4,1)S(1)}, s32[]{:S(2)}) async-start(s8[5505024]{0:T(1024)(128)(4,1)} %bitcast.65), calls=%async_computation.13 | async-start | bytes 8388608
  476.4 20.9 %copy-start.2 = (f32[16,2688]{1,0:T(8,128)S(1)}, f32[16,2688]{1,0:T(8,128)}, u32[]{:S(2)}) copy-start(f32[16,2688]{1,0:T(8,128)} %param.15) | copy-start | bytes 516100
Sparse Core Ops, SparseCore 0:
  125.1 78.1 reduce-scatter.3
  205.8 33.7 reduce-scatter.5
  272.3 124.2 reduce-scatter.7
